TPU v7x, 32 devices: a whole 2x2x4 slice. The times are simulated.
32 devices in a mesh: dp: 8 (over z, x), mp: 4 (over y, core).
Axes of the slice: x: 2, y: 2, z: 4, core: 2. Of those that a mesh axis runs over, the one named last changes fastest.
Arguments:
- hidden_in: bfloat16 [8, 2048, 960], P('dp', 'mp'), may hold values from -6 to 6
- cotangent: bfloat16 [8, 2048, 960], P('dp', 'mp'), may hold values from -6 to 6
- segments: int32 [8, 2048], P('dp'), may hold values from 0 to 3, never falling along the last dimension, each value on 1 to 1024 neighbouring positions
- positions: int32 [8, 2048], P('dp', 'mp'), may hold values from 0 to 4095
- attn_in: bfloat16 [960, 1600], P('dp', 'mp'), may hold values from -0.1875 to 0.1875
- attn_out: bfloat16 [960, 960], P('mp', 'dp'), may hold values from -0.75 to 0.75
- w_gate: bfloat16 [960, 2560], P('dp', 'mp'), may hold values from -0.1875 to 0.1875
- w_up: bfloat16 [960, 2560], P('dp', 'mp'), may hold values from -0.1875 to 0.1875
- w_down: bfloat16 [2560, 960], P('mp', 'dp'), may hold values from -0.125 to 0.125
- norm1_gain: bfloat16 [960], P('dp'), may hold values from 0.099609375 to 1.8984375
- norm2_gain: bfloat16 [960], P('dp'), may hold values from 0.099609375 to 1.8984375
Outputs:
- hidden_out: bfloat16 [8, 2048, 960], P('dp', 'mp')
- grad_hidden: float32 [8, 2048, 960], P('dp', 'mp')
- grad_attn_in: float32 [960, 1600], P('dp', 'mp')
- grad_attn_out: float32 [960, 960], P('mp', 'dp')
- grad_gate: float32 [960, 2560], P('dp', 'mp')
- grad_up: float32 [960, 2560], P('dp', 'mp')
- grad_down: float32 [2560, 960], P('mp', 'dp')
- grad_gain1: float32 [960], P('dp')
- grad_gain2: float32 [960], P('dp')
Inputs may be any that keep to these rules, and one draw needn't show every extreme that they name: `segments`: segment numbers never fall along a sequence; every segment is a run of 1 to 1024 tokens.
All inputs are finite; a program needn't handle non-finite values.
Results may differ from a plain program's by a relative error of at most 0.015.
Values may be sent and summed in bfloat16 or wider, within the bound.
A program may use at most 192 MiB of HBM per device.

v0:
```python
import math
import jax
import jax.numpy as jnp
from jax import lax
from jax.sharding import PartitionSpec as P

HEADS = 15
KV_HEADS = 5
HEAD_DIM = 64
EPSILON = 1e-05
SCORE_SCALE = 0.125
MASK_FILL = -1e30


def rms_forward(values_in, gain):
    inverse = lax.rsqrt(jnp.mean(values_in * values_in, axis=-1, keepdims=True) + EPSILON)
    return (values_in * inverse * gain, inverse)


def rms_backward(values_in, inverse, gain, upstream):
    scaled = upstream * gain
    grad_in = inverse * (
        scaled
        - values_in * inverse * inverse * jnp.mean(scaled * values_in, axis=-1, keepdims=True)
    )
    return (grad_in, jnp.sum(upstream * values_in * inverse, axis=0))


def rotary_tables(position_ids):
    half_dim = HEAD_DIM // 2
    frequency = jnp.exp(
        jnp.arange(half_dim, dtype=jnp.float32) * (-2.0 * math.log(10000.0) / HEAD_DIM)
    )
    angles = position_ids.astype(jnp.float32)[:, None] * frequency[None, :]
    return (jnp.cos(angles)[:, None, :], jnp.sin(angles)[:, None, :])


def rotate(tensor, cosine, sine):
    half_dim = HEAD_DIM // 2
    first, second = (tensor[..., :half_dim], tensor[..., half_dim:])
    return jnp.concatenate(
        [first * cosine - second * sine, second * cosine + first * sine], axis=-1
    )


def rotate_back(tensor, cosine, sine):
    half_dim = HEAD_DIM // 2
    first, second = (tensor[..., :half_dim], tensor[..., half_dim:])
    return jnp.concatenate(
        [first * cosine + second * sine, second * cosine - first * sine], axis=-1
    )


def score_block(queries, keys, allowed):
    scores = (
        jnp.einsum("grd,sd->grs", queries, keys, preferred_element_type=jnp.float32) * SCORE_SCALE
    )
    return jnp.where(allowed[None], scores, MASK_FILL)


def attend(queries, keys, values, allowed):
    scores = score_block(queries, keys, allowed)
    peak = jnp.max(scores, axis=-1, keepdims=True)
    total = jnp.sum(jnp.exp(scores - peak), axis=-1, keepdims=True)
    log_total = peak + jnp.log(total)
    probs = jnp.exp(scores - log_total).astype(jnp.bfloat16)
    output = jnp.einsum("grs,sd->grd", probs, values, preferred_element_type=jnp.float32)
    return (output, log_total[..., 0])


def attend_back(queries, keys, values, allowed, log_total, output_b, grad_out_b):
    scores = score_block(queries, keys, allowed)
    probs = jnp.exp(scores - log_total[..., None])
    probs_b = probs.astype(jnp.bfloat16)
    grad_probs = jnp.einsum("grd,sd->grs", grad_out_b, values, preferred_element_type=jnp.float32)
    delta = jnp.sum(
        grad_out_b.astype(jnp.float32) * output_b.astype(jnp.float32), axis=-1, keepdims=True
    )
    grad_scores = (probs * (grad_probs - delta)).astype(jnp.bfloat16)
    grad_q = (
        jnp.einsum("grs,sd->grd", grad_scores, keys, preferred_element_type=jnp.float32)
        * SCORE_SCALE
    )
    grad_k = (
        jnp.einsum("grs,grd->sd", grad_scores, queries, preferred_element_type=jnp.float32)
        * SCORE_SCALE
    )
    grad_v = jnp.einsum("grs,grd->sd", probs_b, grad_out_b, preferred_element_type=jnp.float32)
    return (grad_q, grad_k, grad_v)


def per_device(
    hidden_in,
    cotangent,
    segments,
    positions,
    attn_in,
    attn_out,
    w_gate,
    w_up,
    w_down,
    norm1_gain,
    norm2_gain,
):
    tok_rows = hidden_in.shape[1]
    model_size = lax.axis_size("mp")
    seq_rows = tok_rows * model_size
    model_rank = lax.axis_index("mp")
    group_size = HEADS // KV_HEADS
    query_cols = HEADS * HEAD_DIM
    kv_cols = KV_HEADS * HEAD_DIM
    gathered = (
        lax.all_gather(attn_in, "dp", axis=0, tiled=True),
        lax.all_gather(attn_out, "dp", axis=1, tiled=True),
        lax.all_gather(w_gate, "dp", axis=0, tiled=True),
        lax.all_gather(w_up, "dp", axis=0, tiled=True),
        lax.all_gather(w_down, "dp", axis=1, tiled=True),
        lax.all_gather(norm1_gain, "dp", axis=0, tiled=True),
        lax.all_gather(norm2_gain, "dp", axis=0, tiled=True),
    )
    qkv_weight, out_weight = (
        lax.all_gather(gathered[0], "mp", axis=1, tiled=True),
        lax.all_gather(gathered[1], "mp", axis=0, tiled=True),
    )
    gate_weight, up_weight, down_weight = (gathered[2], gathered[3], gathered[4])
    gain_one = gathered[5].astype(jnp.float32)
    gain_two = gathered[6].astype(jnp.float32)
    resid_in = hidden_in[0].astype(jnp.float32)
    normed1, inv_one = rms_forward(resid_in, gain_one)
    normed1_b = normed1.astype(jnp.bfloat16)
    projected = jnp.dot(normed1_b, qkv_weight, preferred_element_type=jnp.float32)
    cosine, sine = rotary_tables(positions[0])
    queries = rotate(
        projected[:, :query_cols].reshape(tok_rows, HEADS, HEAD_DIM), cosine, sine
    ).astype(jnp.bfloat16)
    keys_own = (
        rotate(
            projected[:, query_cols : query_cols + kv_cols].reshape(tok_rows, KV_HEADS, HEAD_DIM),
            cosine,
            sine,
        )
        .astype(jnp.bfloat16)
        .reshape(tok_rows, kv_cols)
    )
    values_own = projected[:, query_cols + kv_cols :].astype(jnp.bfloat16)
    keys_all, values_all = (
        lax.all_gather(keys_own, "mp", axis=0, tiled=True),
        lax.all_gather(values_own, "mp", axis=0, tiled=True),
    )
    seq_seg = segments[0]
    query_seg = lax.dynamic_slice_in_dim(seq_seg, model_rank * tok_rows, tok_rows, 0)
    query_index = model_rank * tok_rows + jnp.arange(tok_rows, dtype=jnp.int32)
    key_index = jnp.arange(seq_rows, dtype=jnp.int32)
    allowed = (query_seg[:, None] == seq_seg[None, :]) & (
        key_index[None, :] <= query_index[:, None]
    )
    query_groups = queries.reshape(tok_rows, KV_HEADS, group_size, HEAD_DIM).transpose(1, 2, 0, 3)
    key_groups = keys_all.reshape(seq_rows, KV_HEADS, HEAD_DIM).transpose(1, 0, 2)
    value_groups = values_all.reshape(seq_rows, KV_HEADS, HEAD_DIM).transpose(1, 0, 2)
    outputs, log_totals = lax.map(
        lambda pack: attend(pack[0], pack[1], pack[2], allowed),
        (query_groups, key_groups, value_groups),
    )
    out_groups = outputs.astype(jnp.bfloat16)
    attn_b = out_groups.transpose(2, 0, 1, 3).reshape(tok_rows, query_cols)
    middle = resid_in + jnp.dot(attn_b, out_weight, preferred_element_type=jnp.float32)
    normed2, inv_two = rms_forward(middle, gain_two)
    normed2_b = normed2.astype(jnp.bfloat16)
    seq_normed = lax.all_gather(normed2_b, "mp", axis=0, tiled=True)
    gate = jnp.dot(seq_normed, gate_weight, preferred_element_type=jnp.float32)
    upper = jnp.dot(seq_normed, up_weight, preferred_element_type=jnp.float32)
    sigma = jax.nn.sigmoid(gate)
    silu_gate = gate * sigma
    hidden_b = (silu_gate * upper).astype(jnp.bfloat16)
    ffn_out = lax.psum_scatter(
        jnp.dot(hidden_b, down_weight, preferred_element_type=jnp.float32).astype(jnp.bfloat16),
        "mp",
        scatter_dimension=0,
        tiled=True,
    ).astype(jnp.float32)
    hidden_out = (middle + ffn_out).astype(jnp.bfloat16)
    regathered = (
        lax.all_gather(attn_in, "dp", axis=0, tiled=True),
        lax.all_gather(attn_out, "dp", axis=1, tiled=True),
        lax.all_gather(w_gate, "dp", axis=0, tiled=True),
        lax.all_gather(w_up, "dp", axis=0, tiled=True),
        lax.all_gather(w_down, "dp", axis=1, tiled=True),
        lax.all_gather(norm1_gain, "dp", axis=0, tiled=True),
        lax.all_gather(norm2_gain, "dp", axis=0, tiled=True),
    )
    qkv_weight, out_weight = (
        lax.all_gather(regathered[0], "mp", axis=1, tiled=True),
        lax.all_gather(regathered[1], "mp", axis=0, tiled=True),
    )
    gate_weight, up_weight, down_weight = (regathered[2], regathered[3], regathered[4])
    gain_one = regathered[5].astype(jnp.float32)
    gain_two = regathered[6].astype(jnp.float32)
    cot_local = cotangent[0]
    seq_cot = lax.all_gather(cot_local, "mp", axis=0, tiled=True)
    g_down = jnp.dot(hidden_b.T, seq_cot, preferred_element_type=jnp.float32)
    grad_hid = jnp.dot(seq_cot, down_weight.T, preferred_element_type=jnp.float32)
    grad_gate_act = (grad_hid * upper * sigma * (1.0 + gate * (1.0 - sigma))).astype(jnp.bfloat16)
    grad_up_act = (grad_hid * silu_gate).astype(jnp.bfloat16)
    g_gate = jnp.dot(seq_normed.T, grad_gate_act, preferred_element_type=jnp.float32)
    g_up = jnp.dot(seq_normed.T, grad_up_act, preferred_element_type=jnp.float32)
    grad_norm2 = lax.psum_scatter(
        jnp.dot(grad_gate_act, gate_weight.T, preferred_element_type=jnp.float32)
        + jnp.dot(grad_up_act, up_weight.T, preferred_element_type=jnp.float32),
        "mp",
        scatter_dimension=0,
        tiled=True,
    )
    grad_mid_norm, g_gain2 = rms_backward(middle, inv_two, gain_two, grad_norm2)
    grad_middle = cot_local.astype(jnp.float32) + grad_mid_norm
    middle_b = grad_middle.astype(jnp.bfloat16)
    g_out = jnp.dot(attn_b.T, middle_b, preferred_element_type=jnp.float32)
    grad_attn_b = jnp.dot(middle_b, out_weight.T, preferred_element_type=jnp.float32).astype(
        jnp.bfloat16
    )
    grad_groups = grad_attn_b.reshape(tok_rows, KV_HEADS, group_size, HEAD_DIM).transpose(
        1, 2, 0, 3
    )
    grad_q, grad_k, grad_v = lax.map(
        lambda pack: attend_back(pack[0], pack[1], pack[2], allowed, pack[3], pack[4], pack[5]),
        (query_groups, key_groups, value_groups, log_totals, out_groups, grad_groups),
    )
    key_grads, value_grads = (
        lax.psum_scatter(grad_k, "mp", scatter_dimension=1, tiled=True),
        lax.psum_scatter(grad_v, "mp", scatter_dimension=1, tiled=True),
    )
    grad_q = rotate_back(
        grad_q.transpose(2, 0, 1, 3).reshape(tok_rows, HEADS, HEAD_DIM), cosine, sine
    )
    key_grads = rotate_back(key_grads.transpose(1, 0, 2), cosine, sine)
    value_grads = value_grads.transpose(1, 0, 2)
    grad_proj = jnp.concatenate(
        [
            grad_q.reshape(tok_rows, query_cols),
            key_grads.reshape(tok_rows, kv_cols),
            value_grads.reshape(tok_rows, kv_cols),
        ],
        axis=1,
    ).astype(jnp.bfloat16)
    g_in = jnp.dot(normed1_b.T, grad_proj, preferred_element_type=jnp.float32)
    grad_norm1 = jnp.dot(grad_proj, qkv_weight.T, preferred_element_type=jnp.float32)
    grad_in_norm, g_gain1 = rms_backward(resid_in, inv_one, gain_one, grad_norm1)
    grad_input = grad_middle + grad_in_norm
    reduced = (
        lax.psum_scatter(g_in, "dp", scatter_dimension=0, tiled=True),
        lax.psum_scatter(g_out, "dp", scatter_dimension=1, tiled=True),
        lax.psum_scatter(g_gate, "dp", scatter_dimension=0, tiled=True),
        lax.psum_scatter(g_up, "dp", scatter_dimension=0, tiled=True),
        lax.psum_scatter(g_down, "dp", scatter_dimension=1, tiled=True),
        lax.psum_scatter(g_gain1, "dp", scatter_dimension=0, tiled=True),
        lax.psum_scatter(g_gain2, "dp", scatter_dimension=0, tiled=True),
    )
    grad_attn_in, grad_attn_out = (
        lax.psum_scatter(reduced[0], "mp", scatter_dimension=1, tiled=True),
        lax.psum_scatter(reduced[1], "mp", scatter_dimension=0, tiled=True),
    )
    grad_gain1, grad_gain2 = lax.psum((reduced[5], reduced[6]), "mp")
    return (
        hidden_out[None],
        grad_input[None],
        grad_attn_in,
        grad_attn_out,
        reduced[2],
        reduced[3],
        reduced[4],
        grad_gain1,
        grad_gain2,
    )


def solution(mesh):
    return jax.shard_map(
        per_device,
        mesh=mesh,
        in_specs=(
            P("dp", "mp", None),
            P("dp", "mp", None),
            P("dp", None),
            P("dp", "mp"),
            P("dp", "mp"),
            P("mp", "dp"),
            P("dp", "mp"),
            P("dp", "mp"),
            P("mp", "dp"),
            P("dp"),
            P("dp"),
        ),
        out_specs=(
            P("dp", "mp", None),
            P("dp", "mp", None),
            P("dp", "mp"),
            P("mp", "dp"),
            P("dp", "mp"),
            P("dp", "mp"),
            P("mp", "dp"),
            P("dp"),
            P("dp"),
        ),
        check_vma=False,
    )
```

profile of v0, /device:TPU:0, one launch (start us, length us, event | category | flops | bytes accessed | tf_op | source)
XLA Modules:
  0.0 1195.8 jit_solution(7193035129277229926)
XLA Ops:
  7.3 34.3 %all-gather.1 = bf16[8,120,400]{1,2,0:T(8,128)(2,1)S(1)} all-gather(bf16[1,120,400]{1,2,0:T(8,128)(2,1)} %bitcast.241), channel_id=1, replica_groups=mesh['dp'=8,'mp'=4] {'dp'}, dimensions={0}, use_global_device_ids=true | all-gather | bytes 864000 | tf_op jit(solution)/shard_map/all_gather | solution.py:113
  45.2 21.3 %all-reduce.10 = (bf16[960]{0:T(1024)(128)(2,1)S(1)}, bf16[960]{0:T(1024)(128)(2,1)S(1)}) all-reduce(bf16[960]{0:T(1024)(128)(2,1)S(1)} %dynamic-update-slice, bf16[960]{0:T(1024)(128)(2,1)S(1)} %dynamic-update-slice.1), channel_id=1, replica_groups=mesh['dp'=8,'mp'=4] {'dp'}, use_global_device_ids=true, to_apply=%add | all-reduce | flops 1920 | bytes 7680
  80.2 33.2 %all_gather.53 = bf16[240,960]{0,1:T(8,128)(2,1)} all-gather(bf16[240,120]{0,1:T(8,128)(2,1)S(1)} %copy.27), channel_id=1, replica_groups=mesh['dp'=8,'mp'=4] {'dp'}, dimensions={1}, use_global_device_ids=true | all-gather | bytes 518400 | tf_op jit(solution)/shard_map/all_gather | solution.py:114
  117.5 114.8 %while.30 = (s32[]{:T(128)}, bf16[5,3,512,64]{2,3,1,0:T(8,128)(2,1)S(1)}, f32[5,3,512]{2,1,0:T(4,128)S(1)}, bf16[5,3,512,64]{2,3,1,0:T(8,128)(2,1)S(1)}, bf16[5,...) while((s32[]{:T(128)}, ...), condition=%wide.region_4.5_spmd.clone.clone, body=%wide.region_1.4_spmd.clone.sunk.clone | while | flops 843053568 | bytes 43130984 | solution.py:160
  132.8 8.1 fusion.160
  155.8 8.1 fusion.160
  178.6 8.0 fusion.160
  201.5 8.0 fusion.160
  224.3 8.0 fusion.160
  240.1 30.8 %all-gather.20.cloned.1.call-done = bf16[2048,960]{0,1:T(8,128)(2,1)} async-done(((bf16[512,960]{0,1:T(8,128)(2,1)}), bf16[2048,960]{0,1:T(8,128)(2,1)}) %all-gather.20.cloned.1.call-update) | async-done | bytes 3932176 | tf_op jit(solution)/shard_map/all_gather | solution.py:169
  270.9 8.3 fusion.89
  279.2 35.4 %all-gather.22.cloned.1.call-done = bf16[960,640]{1,0:T(8,128)(2,1)} async-done(((bf16[120,640]{1,0:T(8,128)(2,1)}), bf16[960,640]{1,0:T(8,128)(2,1)}) %all-gather.22.cloned.1.call-update) | async-done | bytes 1228816 | tf_op jit(solution)/shard_map/all_gather | solution.py:115
  314.6 8.3 fusion.88
  322.9 34.1 %all-gather.26.cloned.1.call-done = bf16[640,960]{0,1:T(8,128)(2,1)} async-done(((bf16[640,120]{0,1:T(8,128)(2,1)}), bf16[640,960]{0,1:T(8,128)(2,1)}) %all-gather.26.cloned.1.call-update) | async-done | bytes 1228816 | tf_op jit(solution)/shard_map/all_gather | solution.py:117
  357.0 33.4 %all-gather.28.cloned.1.call-done = bf16[1,2048,960]{1,2,0:T(8,128)(2,1)} async-done(((bf16[1,512,960]{1,2,0:T(8,128)(2,1)}), bf16[1,2048,960]{1,2,0:T(8,128)(2,1)}) %all-gather.28.cloned.1.call-update) | async-done | bytes 3932176 | tf_op jit(solution)/shard_map/all_gather | solution.py:199
  390.4 12.7 %multiply_convert_fusion.1 = (bf16[2048,640]{1,0:T(8,128)(2,1)S(1)}, bf16[2048,640]{1,0:T(8,128)(2,1)S(1)}, bf16[2048,640]{1,0:T(8,128)(2,1)}) fusion(f32[2048,640]{1,0:T(8,128)} %fusion.88, f32[2048,640]{1,0:T(8,128)} %fusion.89, bf16[640,960]{0,1:T(8,128)(2,1)} %all-gather.26.cloned.1.call-done, bf16[1,2048,960]{1,2,0:T(8,128)(2,1)} %all-gather.28.cloned.1.call-done), kind=kOutput, calls=%fused_computation.66 | convolution fusion | flops 2536243200 | bytes 23511040 | tf_op jit(solution)/shard_map/dot_general | solution.py:201
  419.3 61.8 %reduce-scatter.26.cloned.1.call-done = f32[512,960]{0,1:T(8,128)} async-done(((f32[2048,960]{0,1:T(8,128)}), f32[512,960]{0,1:T(8,128)}) %reduce-scatter.26.cloned.1.call-update) | async-done | bytes 1966096 | tf_op jit(solution)/shard_map/reduce_scatter | solution.py:206
  483.8 42.9 %reduce-scatter.24.cloned.1.call-done = bf16[512,960]{0,1:T(8,128)(2,1)} async-done(((bf16[2048,960]{0,1:T(8,128)(2,1)}), bf16[512,960]{0,1:T(8,128)(2,1)}) %reduce-scatter.24.cloned.1.call-update) | async-done | bytes 983056 | tf_op jit(solution)/shard_map/reduce_scatter | solution.py:175
  531.9 101.6 %while.31 = (s32[]{:T(128)}, f32[5,3,512,64]{2,3,1,0:T(8,128)}, f32[5,2048,64]{1,2,0:T(8,128)}, f32[5,2048,64]{1,2,0:T(8,128)}, bf16[5,3,512,64]{2,3,1,0:T(8,128...) while((s32[]{:T(128)}, f32[5,3,512,64]{2,3,1,0:T(8,128)}, ...), condition=%wide.region_11.12_spmd.clone.clone, body=%wide.region_9.11_spmd.clone.sunk.clone | while | flops 2048489984 | bytes 63237260 | solution.py:223
  641.9 26.4 %reduce-scatter.30.cloned.1.call-done = f32[5,512,64]{1,2,0:T(8,128)} async-done(((f32[5,2048,64]{1,2,0:T(8,128)}), f32[5,512,64]{1,2,0:T(8,128)}) %reduce-scatter.30.cloned.1.call-update) | async-done | bytes 655376 | tf_op jit(solution)/shard_map/reduce_scatter | solution.py:229
  670.2 35.5 %reduce-scatter.28.cloned.1.call-done = f32[5,512,64]{1,2,0:T(8,128)} async-done(((f32[5,2048,64]{1,2,0:T(8,128)}), f32[5,512,64]{1,2,0:T(8,128)}) %reduce-scatter.28.cloned.1.call-update) | async-done | bytes 655376 | tf_op jit(solution)/shard_map/reduce_scatter | solution.py:228
  713.0 7.6 fusion.61
  720.7 7.6 fusion.91
  728.4 7.7 fusion.92
  736.1 57.5 %reduce-scatter.36.cloned.1.call-done = f32[120,960]{1,0:T(8,128)} async-done(((f32[960,960]{1,0:T(8,128)}), f32[120,960]{1,0:T(8,128)}) %reduce-scatter.36.cloned.1.call-update) | async-done | bytes 460816
  796.0 122.4 %reduce-scatter.38.cloned.1.call-done = f32[120,1600]{1,0:T(8,128)} async-done(((f32[960,1600]{1,0:T(8,128)}), f32[120,1600]{1,0:T(8,128)}) %reduce-scatter.38.cloned.1.call-update) | async-done | bytes 768016
  927.2 20.1 %all-reduce.8 = (f32[960]{0:T(1024)S(1)}, f32[960]{0:T(1024)S(1)}) all-reduce(f32[960]{0:T(1024)S(1)} %get-tuple-element.203, f32[960]{0:T(1024)S(1)} %copy-done.14), channel_id=14, replica_groups=mesh['dp'=8,'mp'=4] {'dp'}, use_global_device_ids=true, to_apply=%region_23.24.clone | all-reduce | flops 1920 | bytes 15360
  957.3 34.7 %reduce-scatter.44.cloned.1.call-done = f32[640,120]{0,1:T(8,128)} async-done(((f32[640,960]{0,1:T(8,128)}), f32[640,120]{0,1:T(8,128)}) %reduce-scatter.44.cloned.1.call-update) | async-done | bytes 307216
  992.0 73.3 %reduce-scatter.40.cloned.1.call-done = f32[120,640]{1,0:T(8,128)} async-done(((f32[960,640]{1,0:T(8,128)}), f32[120,640]{1,0:T(8,128)}) %reduce-scatter.40.cloned.1.call-update) | async-done | bytes 307216
  1065.3 73.2 %reduce-scatter.42.cloned.1.call-done = f32[120,640]{1,0:T(8,128)} async-done(((f32[960,640]{1,0:T(8,128)}), f32[120,640]{1,0:T(8,128)}) %reduce-scatter.42.cloned.1.call-update) | async-done | bytes 307216
  1138.5 23.6 %reduce-scatter.32.cloned.1.call-done = f32[240,120]{1,0:T(8,128)} async-done(((f32[960,120]{1,0:T(8,128)}), f32[240,120]{1,0:T(8,128)}) %reduce-scatter.32.cloned.1.call-update) | async-done | bytes 115216 | tf_op jit(solution)/shard_map/reduce_scatter | solution.py:259
  1162.1 26.6 %reduce-scatter.34.cloned.1.call-done = f32[400,120]{1,0:T(8,128)} async-done(((f32[1600,120]{1,0:T(8,128)}), f32[400,120]{1,0:T(8,128)}) %reduce-scatter.34.cloned.1.call-update) | async-done | bytes 192016
  (214 shorter events, 265.9 us)
Async XLA Ops:
  7.2 36.2 %copy-start.19 = (u32[32]{0:T(128)S(1)}, u32[32]{0:T(128)}, u32[]{:S(2)}) copy-start(u32[32]{0:T(128)} %constant.80) | copy-start | bytes 388
  7.2 37.6 %copy-start.23 = (bf16[120]{0:T(256)(128)(2,1)S(1)}, bf16[120]{0:T(256)(128)(2,1)}, u32[]{:S(2)}) copy-start(bf16[120]{0:T(256)(128)(2,1)} %param.24) | copy-start | bytes 724
  7.2 37.8 %copy-start.24 = (bf16[120]{0:T(256)(128)(2,1)S(1)}, bf16[120]{0:T(256)(128)(2,1)}, u32[]{:S(2)}) copy-start(bf16[120]{0:T(256)(128)(2,1)} %param.25) | copy-start | bytes 724
  7.2 59.3 %copy-start.5 = (bf16[1,512,960]{1,2,0:T(8,128)(2,1)S(1)}, bf16[1,512,960]{1,2,0:T(8,128)(2,1)}, u32[]{:S(2)}) copy-start(bf16[1,512,960]{1,2,0:T(8,128)(2,1)} %param.15) | copy-start | bytes 2949124
  7.2 66.5 %all-gather.12.cloned.1.call-start = ((), (), s32[]{:S(2)}) async-start(), calls=%async_computation.11 | async-start | bytes 4096000 | tf_op jit(solution)/shard_map/all_gather | solution.py:122
  43.4 74.1 %all-gather.16.cloned.1.call-start = ((), (), s32[]{:S(2)}) async-start(), calls=%async_computation.13 | async-start | bytes 1638400 | tf_op jit(solution)/shard_map/all_gather | solution.py:148
  77.8 37.6 %copy-start.3 = (f32[512,1600]{0,1:T(8,128)}, f32[512,1600]{0,1:T(8,128)S(1)}, u32[]{:S(2)}) copy-start(f32[512,1600]{0,1:T(8,128)S(1)} %fusion.83) | copy-start | bytes 9830404
  78.7 38.8 %all-gather.14.cloned.1.call-start = ((), (), s32[]{:S(2)}) async-start(), calls=%async_computation.12 | async-start | bytes 1638400 | tf_op jit(solution)/shard_map/all_gather | solution.py:147
  79.1 37.4 %copy-start.7 = (f32[512,32]{0,1:T(8,128)}, f32[512,32]{0,1:T(8,128)S(1)}, u32[]{:S(2)}) copy-start(f32[512,32]{0,1:T(8,128)S(1)} %get-tuple-element.272) | copy-start | bytes 196612
  79.1 37.4 %copy-start.9 = (f32[512,32]{0,1:T(8,128)}, f32[512,32]{0,1:T(8,128)S(1)}, u32[]{:S(2)}) copy-start(f32[512,32]{0,1:T(8,128)S(1)} %get-tuple-element.273) | copy-start | bytes 196612
  79.2 37.3 %copy-start.12 = (s32[1,2048]{1,0:T(1,128)S(1)}, s32[1,2048]{1,0:T(1,128)}, u32[]{:S(2)}) copy-start(s32[1,2048]{1,0:T(1,128)} %param.17) | copy-start | bytes 24580
  80.1 152.3 %all-gather.18.cloned.1.call-start = ((), (), s32[]{:S(2)}) async-start(), calls=%async_computation.14 | async-start | bytes 2457600 | tf_op jit(solution)/shard_map/all_gather | solution.py:123
  115.5 124.6 %all-gather.24.cloned.1.call-start = ((), (), s32[]{:S(2)}) async-start(), calls=%async_computation.17 | async-start | bytes 1382400 | tf_op jit(solution)/shard_map/all_gather | solution.py:116
  116.1 154.8 %all-gather.20.cloned.1.call-start = ((), (), s32[]{:S(2)}) async-start(), calls=%async_computation.15 | async-start | bytes 4915200 | tf_op jit(solution)/shard_map/all_gather | solution.py:169
  237.5 77.0 %all-gather.22.cloned.1.call-start = ((), (), s32[]{:S(2)}) async-start(), calls=%async_computation.16 | async-start | bytes 1382400 | tf_op jit(solution)/shard_map/all_gather | solution.py:115
  238.3 118.7 %all-gather.26.cloned.1.call-start = ((), (), s32[]{:S(2)}) async-start(), calls=%async_computation.18 | async-start | bytes 1382400 | tf_op jit(solution)/shard_map/all_gather | solution.py:117
  239.1 151.4 %all-gather.28.cloned.1.call-start = ((), (), s32[]{:S(2)}) async-start(), calls=%async_computation.24 | async-start | bytes 4915200 | tf_op jit(solution)/shard_map/all_gather | solution.py:199
  239.8 241.3 %reduce-scatter.26.cloned.1.call-start = ((), (), s32[]{:S(2)}) async-start(), calls=%async_computation.20 | async-start | bytes 9830400 | tf_op jit(solution)/shard_map/reduce_scatter | solution.py:206
  390.4 12.8 %copy-start.22 = (bf16[960,640]{1,0:T(8,128)(2,1)S(1)}, bf16[960,640]{1,0:T(8,128)(2,1)}, u32[]{:S(2)}) copy-start(bf16[960,640]{1,0:T(8,128)(2,1)} %all-gather.22.cloned.1.call-done) | copy-start | bytes 3686404
  412.0 114.8 %reduce-scatter.24.cloned.1.call-start = ((), (), s32[]{:S(2)}) async-start(), calls=%async_computation.19 | async-start | bytes 4915200 | tf_op jit(solution)/shard_map/reduce_scatter | solution.py:175
  419.2 249.1 %reduce-scatter.30.cloned.1.call-start = ((), (), s32[]{:S(2)}) async-start(), calls=%async_computation.22 | async-start | bytes 3276800 | tf_op jit(solution)/shard_map/reduce_scatter | solution.py:229
  633.5 72.2 %reduce-scatter.28.cloned.1.call-start = ((), (), s32[]{:S(2)}) async-start(), calls=%async_computation.21 | async-start | bytes 3276800 | tf_op jit(solution)/shard_map/reduce_scatter | solution.py:228
  634.2 159.4 %reduce-scatter.36.cloned.1.call-start = ((), (), s32[]{:S(2)}) async-start(), calls=%async_computation.26 | async-start | bytes 4423680
  638.2 280.3 %reduce-scatter.38.cloned.1.call-start = ((), (), s32[]{:S(2)}) async-start(), calls=%async_computation.27 | async-start | bytes 7188480
  640.9 66.1 %copy-start.6 = (bf16[1,512,960]{1,2,0:T(8,128)(2,1)S(1)}, bf16[1,512,960]{1,2,0:T(8,128)(2,1)}, u32[]{:S(2)}) copy-start(bf16[1,512,960]{1,2,0:T(8,128)(2,1)} %param.15) | copy-start | bytes 2949124
  640.9 66.1 %copy-start.16 = (f32[960]{0:T(1024)S(1)}, f32[960]{0:T(1024)}, u32[]{:S(2)}) copy-start(f32[960]{0:T(1024)} %copy-done.15) | copy-start | bytes 11524
  640.9 66.1 %copy-start.18 = (f32[512]{0:T(512)S(1)}, f32[512]{0:T(512)}, u32[]{:S(2)}) copy-start(f32[512]{0:T(512)} %copy-done.17) | copy-start | bytes 6148
  713.0 279.0 %reduce-scatter.44.cloned.1.call-start = ((), (), s32[]{:S(2)}) async-start(), calls=%async_computation.30 | async-start | bytes 2764800
  720.6 344.7 %reduce-scatter.40.cloned.1.call-start = ((), (), s32[]{:S(2)}) async-start(), calls=%async_computation.28 | async-start | bytes 2764800
  728.3 410.2 %reduce-scatter.42.cloned.1.call-start = ((), (), s32[]{:S(2)}) async-start(), calls=%async_computation.29 | async-start | bytes 2764800
  736.0 426.0 %reduce-scatter.32.cloned.1.call-start = ((), (), s32[]{:S(2)}) async-start(), calls=%async_computation.23 | async-start | bytes 614400 | tf_op jit(solution)/shard_map/reduce_scatter | solution.py:259
  795.7 393.0 %reduce-scatter.34.cloned.1.call-start = ((), (), s32[]{:S(2)}) async-start(), calls=%async_computation.25 | async-start | bytes 1024000
  (15 other events, 63.1 us)
Sparse Core Ops, SparseCore 0:
  43.5 30.1 all-gather.11
  78.8 18.1 all-gather.15
  99.2 18.1 all-gather.13
  119.4 21.8 all-gather.17
  143.3 41.4 all-gather.23
  237.7 33.2 all-gather.19
  273.1 41.4 all-gather.21
  316.8 40.2 all-gather.25
  358.6 31.7 all-gather.27
  412.1 68.9 reduce-scatter.25
  483.8 42.8 reduce-scatter.23
  633.6 34.6 reduce-scatter.29
  671.0 34.6 reduce-scatter.27
  709.3 84.3 reduce-scatter.35
  797.5 120.8 reduce-scatter.37
  922.9 69.0 reduce-scatter.43
  996.5 68.8 reduce-scatter.39
  1069.8 68.6 reduce-scatter.41
  1141.7 20.2 reduce-scatter.31
  1165.2 23.4 reduce-scatter.33
where the time goes:
time: 1200 us
  waiting for transfers between devices  722 us (60%)
  matrix products  261 us (22%)
  blocking collectives  115 us (10%)
  other arithmetic  65.6 us (5%)
  between operations  16.4 us (1%)
  local copies, waits for them, and re-layouts  13.4 us (1%)
    unnamed x26, waiting for transfers between devices  391 us
    reduce_scatter x1, waiting for transfers between devices, per_device(): lax.psum_scatter(jnp.dot(grad_gate_act, gate_weight.T, preferred_element_...  61.8 us
    dot_general x10, matrix products, score_block(): jnp.einsum('grd,sd->grs', queries, keys, preferred_element_type=jnp.float32)  48.5 us
    reduce_scatter x1, waiting for transfers between devices, per_device(): lax.psum_scatter(jnp.dot(hidden_b, down_weight, preferred_element_type=jn...  42.9 us
    unnamed x2, blocking collectives  41.4 us
    dot_general x5, matrix products, attend(): jnp.einsum('grs,sd->grd', probs, values, preferred_element_type=jnp.float32)  40.2 us
    reduce_scatter x1, waiting for transfers between devices, per_device(): lax.psum_scatter(grad_k, 'mp', scatter_dimension=1, tiled=True)  35.5 us
    all_gather x1, waiting for transfers between devices, per_device(): lax.all_gather(w_gate, 'dp', axis=0, tiled=True)  35.4 us
  transfers between devices with their start and end apart: 20, of which 16 were waited for; matrix products, arithmetic and copies ran while one was open for 17% of the time, Pallas kernels for 0%

commit v1 on v0

--- a/solution.py
+++ b/solution.py
@@ -10,6 +10,17 @@
 EPSILON = 1e-05
 SCORE_SCALE = 0.125
 MASK_FILL = -1e30
+
+
+def collect(x, axis, dim):
+    ways = lax.axis_size(axis)
+    pieces = [x]
+    for far in range(1, ways):
+        pieces.append(
+            lax.ppermute(pieces[far - 1], axis, [(d, (d - 1) % ways) for d in range(ways)])
+        )
+    line = jnp.concatenate(pieces, axis=dim)
+    return jnp.roll(line, lax.axis_index(axis) * x.shape[dim], axis=dim)
 
 
 def rms_forward(values_in, gain):
@@ -112,7 +123,7 @@
     gathered = (
         lax.all_gather(attn_in, "dp", axis=0, tiled=True),
         lax.all_gather(attn_out, "dp", axis=1, tiled=True),
-        lax.all_gather(w_gate, "dp", axis=0, tiled=True),
+        collect(w_gate, "dp", 0),
         lax.all_gather(w_up, "dp", axis=0, tiled=True),
         lax.all_gather(w_down, "dp", axis=1, tiled=True),
         lax.all_gather(norm1_gain, "dp", axis=0, tiled=True),

time: 1200 us -> 1140 us (0.950)
  waiting for transfers between devices: 722 us -> 612 us
  starting transfers between devices: 1.66 us -> 36.7 us
  local copies, waits for them, and re-layouts: 13.4 us -> 31.8 us
    ppermute x0 -> x7, starting transfers between devices: none -> 35.2 us  [collect(): lax.ppermute(pieces[far - 1], axis, [(d, (d - 1) % ways) for d in range(w...]
    all_gather x1, waiting for transfers between devices: 34.1 us -> 0.01 us  [per_device(): lax.all_gather(w_down, 'dp', axis=1, tiled=True)]
    all_gather x1, waiting for transfers between devices: 33.4 us -> 0.01 us  [per_device(): seq_cot = lax.all_gather(cot_local, 'mp', axis=0, tiled=True)]
    all_gather x1, waiting for transfers between devices: 30.8 us -> 0.01 us  [per_device(): seq_normed = lax.all_gather(normed2_b, 'mp', axis=0, tiled=True)]
    all_gather x1, waiting for transfers between devices: 35.4 us -> 6.5 us  [per_device(): lax.all_gather(w_gate, 'dp', axis=0, tiled=True)]
    ppermute x0 -> x7, waiting for transfers between devices: none -> 20.3 us  [collect(): lax.ppermute(pieces[far - 1], axis, [(d, (d - 1) % ways) for d in range(w...]
    unnamed x63 -> x90, local copies, waits for them, and re-layouts: 9.75 us -> 26.6 us
  transfers between devices with their start and end apart: 20 -> 27, of which waited for: 16 -> 18; matrix products, arithmetic and copies ran while one was open for 17% -> 20% of each run, Pallas kernels for 0% -> 0%
where the time goes in v1:
time: 1140 us
  waiting for transfers between devices  612 us (54%)
  matrix products  258 us (23%)
  blocking collectives  115 us (10%)
  other arithmetic  65.3 us (6%)
  starting transfers between devices  36.7 us (3%)
  local copies, waits for them, and re-layouts  31.8 us (3%)
  between operations  16.5 us (1%)
    unnamed x26, waiting for transfers between devices  390 us
    reduce_scatter x1, waiting for transfers between devices, per_device(): lax.psum_scatter(jnp.dot(grad_gate_act, gate_weight.T, preferred_element_...  60.6 us
    dot_general x10, matrix products, score_block(): jnp.einsum('grd,sd->grs', queries, keys, preferred_element_type=jnp.float32)  49 us
    reduce_scatter x1, waiting for transfers between devices, per_device(): lax.psum_scatter(jnp.dot(hidden_b, down_weight, preferred_element_type=jn...  42.9 us
    unnamed x2, blocking collectives  41.4 us
    dot_general x5, matrix products, attend(): jnp.einsum('grs,sd->grd', probs, values, preferred_element_type=jnp.float32)  40.5 us
    reduce_scatter x1, waiting for transfers between devices, per_device(): lax.psum_scatter(grad_k, 'mp', scatter_dimension=1, tiled=True)  35.6 us
    ppermute x7, starting transfers between devices, collect(): lax.ppermute(pieces[far - 1], axis, [(d, (d - 1) % ways) for d in range(w...  35.2 us
  transfers between devices with their start and end apart: 27, of which 18 were waited for; matrix products, arithmetic and copies ran while one was open for 20% of the time, Pallas kernels for 0%

profile of v1, /device:TPU:0, one launch (start us, length us, event | category | flops | bytes accessed | tf_op | source)
XLA Modules:
  0.0 1136.7 jit_solution(12551509302215066943)
XLA Ops:
  7.3 34.3 %all-gather.1 = bf16[8,120,400]{1,2,0:T(8,128)(2,1)S(1)} all-gather(bf16[1,120,400]{1,2,0:T(8,128)(2,1)} %bitcast.238), channel_id=1, replica_groups=mesh['dp'=8,'mp'=4] {'dp'}, dimensions={0}, use_global_device_ids=true | all-gather | bytes 864000 | tf_op jit(solution)/shard_map/all_gather | solution.py:124
  45.2 21.3 %all-reduce.10 = (bf16[960]{0:T(1024)(128)(2,1)S(1)}, bf16[960]{0:T(1024)(128)(2,1)S(1)}) all-reduce(bf16[960]{0:T(1024)(128)(2,1)S(1)} %dynamic-update-slice, bf16[960]{0:T(1024)(128)(2,1)S(1)} %dynamic-update-slice.1), channel_id=1, replica_groups=mesh['dp'=8,'mp'=4] {'dp'}, use_global_device_ids=true, to_apply=%add | all-reduce | flops 1920 | bytes 7680
  66.8 6.9 all-gather.12.cloned.1.call-done
  80.2 33.2 %all_gather.52 = bf16[240,960]{0,1:T(8,128)(2,1)} all-gather(bf16[240,120]{0,1:T(8,128)(2,1)S(1)} %copy.27), channel_id=1, replica_groups=mesh['dp'=8,'mp'=4] {'dp'}, dimensions={1}, use_global_device_ids=true | all-gather | bytes 518400 | tf_op jit(solution)/shard_map/all_gather | solution.py:125
  119.6 115.1 %while.30 = (s32[]{:T(128)}, bf16[5,3,512,64]{2,3,1,0:T(8,128)(2,1)S(1)}, f32[5,3,512]{2,1,0:T(4,128)S(1)}, bf16[5,3,512,64]{2,3,1,0:T(8,128)(2,1)S(1)}, bf16[5,...) while((s32[]{:T(128)}, ...), condition=%wide.region_4.5_spmd.clone.clone, body=%wide.region_1.4_spmd.clone.sunk.clone | while | flops 843053568 | bytes 43130984 | solution.py:171
  120.8 7.0 fusion.160
  134.6 8.1 fusion.161
  150.7 6.8 exponential_reduce_fusion.3
  157.6 8.1 fusion.161
  180.5 8.0 fusion.161
  189.7 7.1 fusion.160
  203.7 8.1 fusion.161
  226.6 8.2 fusion.161
  313.3 8.3 fusion.63
  327.7 9.4 multiply_convert_fusion.1
  354.5 7.2 convolution_convert_fusion
  361.8 60.6 %reduce-scatter.26.cloned.1.call-done = f32[512,960]{0,1:T(8,128)} async-done(((f32[2048,960]{0,1:T(8,128)}), f32[512,960]{0,1:T(8,128)}) %reduce-scatter.26.cloned.1.call-update) | async-done | bytes 1966096 | tf_op jit(solution)/shard_map/reduce_scatter | solution.py:217
  425.1 42.9 %reduce-scatter.24.cloned.1.call-done = bf16[512,960]{0,1:T(8,128)(2,1)} async-done(((bf16[2048,960]{0,1:T(8,128)(2,1)}), bf16[512,960]{0,1:T(8,128)(2,1)}) %reduce-scatter.24.cloned.1.call-update) | async-done | bytes 983056 | tf_op jit(solution)/shard_map/reduce_scatter | solution.py:186
  473.2 101.7 %while.31 = (s32[]{:T(128)}, f32[5,3,512,64]{2,3,1,0:T(8,128)}, f32[5,2048,64]{1,2,0:T(8,128)}, f32[5,2048,64]{1,2,0:T(8,128)}, bf16[5,3,512,64]{2,3,1,0:T(8,128...) while((s32[]{:T(128)}, f32[5,3,512,64]{2,3,1,0:T(8,128)}, ...), condition=%wide.region_11.12_spmd.clone.clone, body=%wide.region_9.11_spmd.clone.sunk.clone | while | flops 2048489984 | bytes 63237260 | solution.py:234
  583.4 26.4 %reduce-scatter.30.cloned.1.call-done = f32[5,512,64]{1,2,0:T(8,128)} async-done(((f32[5,2048,64]{1,2,0:T(8,128)}), f32[5,512,64]{1,2,0:T(8,128)}) %reduce-scatter.30.cloned.1.call-update) | async-done | bytes 655376 | tf_op jit(solution)/shard_map/reduce_scatter | solution.py:240
  611.6 35.6 %reduce-scatter.28.cloned.1.call-done = f32[5,512,64]{1,2,0:T(8,128)} async-done(((f32[5,2048,64]{1,2,0:T(8,128)}), f32[5,512,64]{1,2,0:T(8,128)}) %reduce-scatter.28.cloned.1.call-update) | async-done | bytes 655376 | tf_op jit(solution)/shard_map/reduce_scatter | solution.py:239
  654.5 7.6 fusion.61
  662.2 7.6 fusion.93
  669.9 7.7 fusion.94
  677.7 57.4 %reduce-scatter.36.cloned.1.call-done = f32[120,960]{1,0:T(8,128)} async-done(((f32[960,960]{1,0:T(8,128)}), f32[120,960]{1,0:T(8,128)}) %reduce-scatter.36.cloned.1.call-update) | async-done | bytes 460816
  737.4 122.4 %reduce-scatter.38.cloned.1.call-done = f32[120,1600]{1,0:T(8,128)} async-done(((f32[960,1600]{1,0:T(8,128)}), f32[120,1600]{1,0:T(8,128)}) %reduce-scatter.38.cloned.1.call-update) | async-done | bytes 768016
  868.6 20.1 %all-reduce.8 = (f32[960]{0:T(1024)S(1)}, f32[960]{0:T(1024)S(1)}) all-reduce(f32[960]{0:T(1024)S(1)} %get-tuple-element.203, f32[960]{0:T(1024)S(1)} %copy-done.20), channel_id=14, replica_groups=mesh['dp'=8,'mp'=4] {'dp'}, use_global_device_ids=true, to_apply=%region_23.24.clone | all-reduce | flops 1920 | bytes 15360
  898.8 34.4 %reduce-scatter.44.cloned.1.call-done = f32[640,120]{0,1:T(8,128)} async-done(((f32[640,960]{0,1:T(8,128)}), f32[640,120]{0,1:T(8,128)}) %reduce-scatter.44.cloned.1.call-update) | async-done | bytes 307216
  933.2 73.1 %reduce-scatter.40.cloned.1.call-done = f32[120,640]{1,0:T(8,128)} async-done(((f32[960,640]{1,0:T(8,128)}), f32[120,640]{1,0:T(8,128)}) %reduce-scatter.40.cloned.1.call-update) | async-done | bytes 307216
  1006.3 73.1 %reduce-scatter.42.cloned.1.call-done = f32[120,640]{1,0:T(8,128)} async-done(((f32[960,640]{1,0:T(8,128)}), f32[120,640]{1,0:T(8,128)}) %reduce-scatter.42.cloned.1.call-update) | async-done | bytes 307216
  1079.4 23.6 %reduce-scatter.32.cloned.1.call-done = f32[240,120]{1,0:T(8,128)} async-done(((f32[960,120]{1,0:T(8,128)}), f32[240,120]{1,0:T(8,128)}) %reduce-scatter.32.cloned.1.call-update) | async-done | bytes 115216 | tf_op jit(solution)/shard_map/reduce_scatter | solution.py:270
  1103.0 26.6 %reduce-scatter.34.cloned.1.call-done = f32[400,120]{1,0:T(8,128)} async-done(((f32[1600,120]{1,0:T(8,128)}), f32[400,120]{1,0:T(8,128)}) %reduce-scatter.34.cloned.1.call-update) | async-done | bytes 192016
  (256 shorter events, 318.8 us)
Async XLA Ops:
  7.2 66.5 %all-gather.12.cloned.1.call-start = ((), (), s32[]{:S(2)}) async-start(), calls=%async_computation.11 | async-start | bytes 4096000 | tf_op jit(solution)/shard_map/all_gather | solution.py:133
  7.3 59.3 %copy-start.5 = (bf16[1,512,960]{1,2,0:T(8,128)(2,1)S(1)}, bf16[1,512,960]{1,2,0:T(8,128)(2,1)}, u32[]{:S(2)}) copy-start(bf16[1,512,960]{1,2,0:T(8,128)(2,1)} %param.15) | copy-start | bytes 2949124
  43.4 76.2 %all-gather.16.cloned.1.call-start = ((), (), s32[]{:S(2)}) async-start(), calls=%async_computation.13 | async-start | bytes 1638400 | tf_op jit(solution)/shard_map/all_gather | solution.py:159
  78.7 40.9 %all-gather.14.cloned.1.call-start = ((), (), s32[]{:S(2)}) async-start(), calls=%async_computation.12 | async-start | bytes 1638400 | tf_op jit(solution)/shard_map/all_gather | solution.py:158
  80.0 154.8 %all-gather.18.cloned.1.call-start = ((), (), s32[]{:S(2)}) async-start(), calls=%async_computation.14 | async-start | bytes 2457600 | tf_op jit(solution)/shard_map/all_gather | solution.py:134
  115.4 197.8 %all-gather.24.cloned.1.call-start = ((), (), s32[]{:S(2)}) async-start(), calls=%async_computation.17 | async-start | bytes 1382400 | tf_op jit(solution)/shard_map/all_gather | solution.py:128
  116.0 197.3 %all-gather.28.cloned.1.call-start = ((), (), s32[]{:S(2)}) async-start(), calls=%async_computation.24 | async-start | bytes 4915200 | tf_op jit(solution)/shard_map/all_gather | solution.py:210
  116.6 205.0 %all-gather.22.cloned.1.call-start = ((), (), s32[]{:S(2)}) async-start(), calls=%async_computation.16 | async-start | bytes 1382400 | tf_op jit(solution)/shard_map/all_gather | solution.py:127
  117.4 204.2 %all-gather.20.cloned.1.call-start = ((), (), s32[]{:S(2)}) async-start(), calls=%async_computation.15 | async-start | bytes 4915200 | tf_op jit(solution)/shard_map/all_gather | solution.py:180
  240.0 103.6 %all-gather.26.cloned.1.call-start = ((), (), s32[]{:S(2)}) async-start(), calls=%async_computation.19 | async-start | bytes 1382400 | tf_op jit(solution)/shard_map/all_gather | solution.py:196
  240.1 10.3 collective-permute-start
  251.0 11.2 collective-permute-start.1
  256.2 50.5 %copy-start.16 = (bf16[120,640]{1,0:T(8,128)(2,1)S(1)}, bf16[120,640]{1,0:T(8,128)(2,1)}, u32[]{:S(2)}) copy-start(bf16[120,640]{1,0:T(8,128)(2,1)} %copy-done.15) | copy-start | bytes 460804
  262.9 9.4 collective-permute-start.2
  272.3 9.0 collective-permute-start.3
  277.6 144.8 %reduce-scatter.26.cloned.1.call-start = ((), (), s32[]{:S(2)}) async-start(), calls=%async_computation.20 | async-start | bytes 9830400 | tf_op jit(solution)/shard_map/reduce_scatter | solution.py:217
  281.3 8.3 collective-permute-start.4
  289.6 8.1 collective-permute-start.5
  297.8 7.6 collective-permute-start.6
  354.5 113.6 %reduce-scatter.24.cloned.1.call-start = ((), (), s32[]{:S(2)}) async-start(), calls=%async_computation.18 | async-start | bytes 4915200 | tf_op jit(solution)/shard_map/reduce_scatter | solution.py:186
  361.7 248.0 %reduce-scatter.30.cloned.1.call-start = ((), (), s32[]{:S(2)}) async-start(), calls=%async_computation.22 | async-start | bytes 3276800 | tf_op jit(solution)/shard_map/reduce_scatter | solution.py:240
  574.9 72.3 %reduce-scatter.28.cloned.1.call-start = ((), (), s32[]{:S(2)}) async-start(), calls=%async_computation.21 | async-start | bytes 3276800 | tf_op jit(solution)/shard_map/reduce_scatter | solution.py:239
  575.6 159.4 %reduce-scatter.36.cloned.1.call-start = ((), (), s32[]{:S(2)}) async-start(), calls=%async_computation.26 | async-start | bytes 4423680
  579.5 280.2 %reduce-scatter.38.cloned.1.call-start = ((), (), s32[]{:S(2)}) async-start(), calls=%async_computation.27 | async-start | bytes 7188480
  582.3 66.1 %copy-start.6 = (bf16[1,512,960]{1,2,0:T(8,128)(2,1)S(1)}, bf16[1,512,960]{1,2,0:T(8,128)(2,1)}, u32[]{:S(2)}) copy-start(bf16[1,512,960]{1,2,0:T(8,128)(2,1)} %param.15) | copy-start | bytes 2949124
  582.3 66.1 %copy-start.22 = (f32[960]{0:T(1024)S(1)}, f32[960]{0:T(1024)}, u32[]{:S(2)}) copy-start(f32[960]{0:T(1024)} %copy-done.21) | copy-start | bytes 11524
  582.3 66.1 %copy-start.24 = (f32[512]{0:T(512)S(1)}, f32[512]{0:T(512)}, u32[]{:S(2)}) copy-start(f32[512]{0:T(512)} %copy-done.23) | copy-start | bytes 6148
  654.5 278.7 %reduce-scatter.44.cloned.1.call-start = ((), (), s32[]{:S(2)}) async-start(), calls=%async_computation.30 | async-start | bytes 2764800
  662.1 344.2 %reduce-scatter.40.cloned.1.call-start = ((), (), s32[]{:S(2)}) async-start(), calls=%async_computation.28 | async-start | bytes 2764800
  669.8 409.5 %reduce-scatter.42.cloned.1.call-start = ((), (), s32[]{:S(2)}) async-start(), calls=%async_computation.29 | async-start | bytes 2764800
  677.6 425.4 %reduce-scatter.32.cloned.1.call-start = ((), (), s32[]{:S(2)}) async-start(), calls=%async_computation.23 | async-start | bytes 614400 | tf_op jit(solution)/shard_map/reduce_scatter | solution.py:270
  737.1 392.5 %reduce-scatter.34.cloned.1.call-start = ((), (), s32[]{:S(2)}) async-start(), calls=%async_computation.25 | async-start | bytes 1024000
  (28 other events, 409.8 us)
Sparse Core Ops, SparseCore 0:
  43.5 30.1 all-gather.11
  78.8 18.1 all-gather.15
  99.2 18.1 all-gather.13
  119.4 21.8 all-gather.17
  143.3 41.4 all-gather.23
  186.2 31.8 all-gather.27
  220.2 45.8 all-gather.21
  268.3 31.6 all-gather.19
  302.1 41.4 all-gather.25
  354.6 67.7 reduce-scatter.25
  425.1 42.8 reduce-scatter.23
  575.0 34.6 reduce-scatter.29
  612.4 34.6 reduce-scatter.27
  650.7 84.2 reduce-scatter.35
  738.9 120.8 reduce-scatter.37
  864.3 68.9 reduce-scatter.43
  937.7 68.5 reduce-scatter.39
  1010.8 68.5 reduce-scatter.41
  1082.6 20.2 reduce-scatter.31
  1106.1 23.4 reduce-scatter.33
